TPU v7x, 256 devices: a whole 4x4x8 slice. The times are simulated.
256 devices in a mesh: leaf: 256 (over x, z, y, core).
Axes of the slice: x: 4, y: 4, z: 8, core: 2. Of those that a mesh axis runs over, the one named last changes fastest.
Arguments:
- points: bfloat16 [128, 2097152], P(None, 'leaf')
- probes: bfloat16 [16, 2097152], P(None, 'leaf'), may hold values from -6 to 6
- near_list: int32 [4096, 4], P('leaf'), may hold values from 0 to 4095, as said below
- near_count: int32 [4096], P('leaf'), may hold values from 1 to 4, as said below
- leaf_skel: int32 [4096, 128], P('leaf'), may hold values from 0 to 511, as said below
- local_skel: int32 [3840, 128], P('leaf'), may hold values from 0 to 255, as said below
- upper_skel: int32 [255, 128], replicated, may hold values from 0 to 255, as said below
Outputs:
- response: float32 [16, 2097152], P(None, 'leaf')
Inputs may be any that keep to these rules, and one draw needn't show every extreme that they name: `near_list`: entry 0 of leaf t's list is t itself; every entry is a leaf of the same block of 16 consecutive leaves as t, or of the block just before or just after it. `near_count`: some leaf uses all 4 slots. `leaf_skel`: each row holds 128 distinct values. `local_skel`: each row holds 128 distinct values. `upper_skel`: each row holds 128 distinct values.
All inputs are finite; a program needn't handle non-finite values.
Results may differ from a plain program's by a relative error of at most 0.0015.
Values may be sent and summed in bfloat16 or wider, within the bound.
No kernel may reach another device: no remote copies, remote signals or barrier semaphores. Data moves between devices by JAX's collectives and lax.ppermute only.
A program may use at most 128 MiB of HBM per device.

v0:
```python
import functools
import math

import jax
import jax.numpy as jnp
from jax import lax
from jax.experimental import pallas as pl
from jax.experimental.pallas import tpu as pltpu
from jax.sharding import PartitionSpec as P


F32 = jnp.float32
BF16 = jnp.bfloat16
AUG = 16
SQ_TOP = 3.0e38
VMEM_MIB = 20
GROUP = 8
NEAR_TILE = 512
CHIP_PARTS = 4
SENDS = {2: (0,), 3: (1,), 4: (2,), 5: (3,)}
SUMS = {
    2: (2, (-1,)),
    3: (3, (-1,)),
    4: (4, (-1, 0)),
    5: (12, (-1, 0, 1)),
    6: (4, (-1, 0, 1, 2)),
    7: (None, (-1, 0, 1, 2, 3)),
}


def mm(a, b):
    return lax.dot_general(a, b, (((1,), (0,)), ((), ())), preferred_element_type=F32)


def mm_nt(a, b):
    return lax.dot_general(a, b, (((1,), (1,)), ((), ())), preferred_element_type=F32)


def mm_tn(a, b):
    return lax.dot_general(a, b, (((0,), (0,)), ((), ())), preferred_element_type=F32)


def halves(x):
    high = x.astype(BF16)
    return high, (x - high.astype(F32)).astype(BF16)


def square_rows(pts):
    wide = pts.astype(F32)
    sq = jnp.sum(wide * wide, axis=0, keepdims=True)
    neg = -0.5 * jnp.minimum(sq, SQ_TOP)
    one = neg.astype(BF16).astype(F32)
    rest = neg - one
    two = rest.astype(BF16).astype(F32)
    three = rest - two
    return one, two, three


def aug_rows(pieces, left, width):
    one, two, three = pieces
    row = lax.broadcasted_iota(jnp.int32, (AUG, width), 0)
    if not left:
        row = jnp.where(row < 3, row + 3, jnp.where(row < 6, row - 3, row))
    ones = jnp.where((row >= 3) & (row < 6), 1.0, 0.0)
    body = jnp.where(row == 0, one, jnp.where(row == 1, two, jnp.where(row == 2, three, ones)))
    return body.astype(BF16)


def exp_scaled(z, emb):
    return jnp.exp2(z * (4.0 / emb * math.log2(math.e)))


def affinity(left, right, emb):
    return exp_scaled(mm_tn(left, right), emb)


def left_of(ext, emb):
    return ext[: emb + AUG]


def right_of(ext, emb):
    return jnp.concatenate([ext[:emb], ext[emb + AUG : emb + 2 * AUG]], axis=0)


def one_hot(chosen, pool):
    ids = lax.broadcasted_iota(jnp.int32, (pool, chosen.shape[1]), 0)
    return jnp.where(ids == chosen, 1.0, 0.0).astype(BF16)


def up_kernel(emb, leaf_num, leaf_len, group, all_ref, leaf_skel_ref, local_skel_ref,
              root_ref, leaf_ref, tree_ref, couple_ref, left_ref, node_ref):
    skel_len = leaf_skel_ref.shape[1]
    ext_rows = emb + 2 * AUG

    def leaf_step(step, carry):
        ids = [step * group + k for k in range(group)]
        cols = [pl.ds(pl.multiple_of(leaf * leaf_len, leaf_len), leaf_len) for leaf in ids]
        hots = [one_hot(leaf_skel_ref[pl.ds(leaf, 1), :], leaf_len) for leaf in ids]
        exts = []
        for at in cols:
            pts = all_ref[:emb, at]
            pieces = square_rows(pts)
            exts.append(jnp.concatenate(
                [pts, aug_rows(pieces, True, leaf_len), aug_rows(pieces, False, leaf_len)], axis=0))
        skels = [mm(ext, hot).astype(BF16) for ext, hot in zip(exts, hots)]
        zs = [mm_tn(left_of(skel, emb), right_of(ext, emb)) for skel, ext in zip(skels, exts)]
        lefts = [left_of(ext, emb).T for ext in exts]
        pairs = [halves(exp_scaled(z, emb)) for z in zs]
        charges = [
            (mm_nt(all_ref[emb:, at], high) + mm_nt(all_ref[emb:, at], low)).astype(BF16)
            for at, (high, low) in zip(cols, pairs)
        ]
        for leaf, left, skel, charge, (high, low) in zip(ids, lefts, skels, charges, pairs):
            left_ref[leaf] = left
            node_ref[leaf, :ext_rows, :] = skel
            node_ref[leaf, ext_rows:, :] = charge
            leaf_ref[leaf, :skel_len, :] = high
            leaf_ref[leaf, skel_len:, :] = low
        return carry

    lax.fori_loop(0, leaf_num // group, leaf_step, 0)

    start, row = 0, 0
    width = leaf_num // 2
    while width >= 1:
        part = min(width, group)
        for base in range(0, width, part):
            ks = range(base, base + part)
            hots = [one_hot(local_skel_ref[row + k : row + k + 1, :], 2 * skel_len) for k in ks]
            kids = [(node_ref[start + 2 * k], node_ref[start + 2 * k + 1]) for k in ks]
            exts = [(x[:ext_rows], y[:ext_rows]) for x, y in kids]
            qs = [(x[ext_rows:], y[ext_rows:]) for x, y in kids]
            joins = [jnp.concatenate(pair, axis=1) for pair in exts]
            parents = [mm(joined, hot).astype(BF16) for joined, hot in zip(joins, hots)]
            crosses = [mm_tn(left_of(x, emb), right_of(y, emb)) for x, y in exts]
            zs = [mm_tn(left_of(parent, emb), right_of(joined, emb))
                  for parent, joined in zip(parents, joins)]
            crosses = [halves(exp_scaled(z, emb)) for z in crosses]
            pairs = [halves(exp_scaled(z, emb)) for z in zs]
            parent_qs = []
            for (x, y), (high, low) in zip(qs, pairs):
                joined_q = jnp.concatenate([x, y], axis=1)
                parent_qs.append((mm_nt(joined_q, high) + mm_nt(joined_q, low)).astype(BF16))
            for k, (x, y), (high, low) in zip(ks, qs, crosses):
                couple_ref[row + k, :, :skel_len] = mm_nt(y, high) + mm_nt(y, low)
                couple_ref[row + k, :, skel_len:] = mm(x, high) + mm(x, low)
            for k, parent, parent_q, (high, low) in zip(ks, parents, parent_qs, pairs):
                tree_ref[row + k, :skel_len, :] = high
                tree_ref[row + k, skel_len:, :] = low
                target = start + 2 * width + k
                node_ref[target, :ext_rows, :] = parent
                node_ref[target, ext_rows:, :] = parent_q
        start, row, width = start + 2 * width, row + width, width // 2
    root_ref[...] = node_ref[start]


def level_kernel(emb, cur_ref, sib_ref, chosen_ref, couple_ref, own_ref, next_ref=None):
    skel_len = chosen_ref.shape[1]
    ext_rows = emb + 2 * AUG
    cur, sib = cur_ref[...], sib_ref[...]
    cur_ext, cur_q = cur[:ext_rows], cur[ext_rows:]
    sib_ext, sib_q = sib[:ext_rows], sib[ext_rows:]
    joined = jnp.concatenate([cur_ext, sib_ext], axis=1)
    joined_q = jnp.concatenate([cur_q, sib_q], axis=1)
    hot = one_hot(chosen_ref[...], 2 * skel_len)
    parent = mm(joined, hot).astype(BF16)
    high, low = halves(affinity(left_of(parent, emb), right_of(joined, emb), emb))
    if next_ref is not None:
        next_ref[:ext_rows, :] = parent
        next_ref[ext_rows:, :] = (mm_nt(joined_q, high) + mm_nt(joined_q, low)).astype(BF16)
    own_ref[:skel_len, :] = high[:, :skel_len]
    own_ref[skel_len:, :] = low[:, :skel_len]
    high, low = halves(affinity(left_of(sib_ext, emb), right_of(cur_ext, emb), emb))
    couple_ref[...] = mm(sib_q, high) + mm(sib_q, low)


def near_sum(leaf_len, bucket, first, last, lists_ref, left_ref, pts_ref, prb_ref, out_ref):
    tile = min(NEAR_TILE, leaf_len)
    emb = pts_ref.shape[0]

    def step(item, carry):
        leaf = lists_ref[2 * bucket, item]
        place = lists_ref[2 * bucket + 1, item]
        cols = pl.ds(pl.multiple_of(place * leaf_len, leaf_len), leaf_len)
        pts = pts_ref[:, cols]
        right = jnp.concatenate([pts, aug_rows(square_rows(pts), False, leaf_len)], axis=0)
        prb = prb_ref[:, cols]
        starts = list(range(0, leaf_len, tile))
        terms, ahead, kern = [], mm(left_ref[leaf, :tile, :], right), None
        for n in range(len(starts)):
            z = ahead
            if n + 1 < len(starts):
                ahead = mm(left_ref[leaf, starts[n + 1] : starts[n + 1] + tile, :], right)
            last, kern = kern, exp_scaled(z, emb).astype(BF16)
            if n > 0:
                terms.append(mm_nt(prb, last))
        terms.append(mm_nt(prb, kern))
        at = pl.ds(pl.multiple_of(leaf * leaf_len, leaf_len), leaf_len)
        out_ref[:, at] += jnp.concatenate(terms, axis=1)
        return carry

    lax.fori_loop(first, last, step, 0)


def near_own_kernel(emb, leaf_len, chip_span, ids_ref, count_ref, left_ref, all_ref,
                    out_ref, lists_ref):
    leaf_num = count_ref.shape[0]
    bucket_num = lists_ref.shape[0] // 2
    unused, lengths = bucket_num - 1, 2 * bucket_num
    out_ref[...] = jnp.zeros_like(out_ref)
    for bucket in range(bucket_num):
        lists_ref[lengths, bucket] = 0

    def scan_leaf(leaf, carry):
        count = count_ref[leaf]
        for slot in range(ids_ref.shape[1]):
            source = ids_ref[leaf, slot]
            on_link = source < leaf_num
            on_chip = source >= 2 * leaf_num
            home = source - jnp.where(on_link, 0, jnp.where(on_chip, 2 * leaf_num, leaf_num))
            part = jnp.where(on_chip, lax.div(home, chip_span), 0)
            bucket = jnp.where(on_link, 1, jnp.where(on_chip, 2 + part, 0))
            bucket = jnp.where(slot < count, bucket, unused)
            filled = lists_ref[lengths, bucket]
            lists_ref[2 * bucket, filled] = leaf
            lists_ref[2 * bucket + 1, filled] = home - part * chip_span
            lists_ref[lengths, bucket] = filled + 1
        return carry

    lax.fori_loop(0, leaf_num, scan_leaf, 0, unroll=4)
    near_sum(leaf_len, 0, 0, lists_ref[lengths, 0], lists_ref, left_ref,
             all_ref.at[:emb], all_ref.at[emb:], out_ref)


def near_kernel(emb, leaf_len, turns, lists_ref, left_ref, *refs):
    _, out_ref = refs[-2:]
    lengths = lists_ref.shape[0] - 1
    done = {}
    for turn, (budget, buckets) in enumerate(turns):
        for bucket, src_ref in zip(buckets, refs[:-2]):
            first = done.get(bucket, 0)
            count = lists_ref[lengths, bucket] - first
            if budget is not None:
                count = jnp.minimum(count, budget)
                budget = budget - count
            done[bucket] = first + count
            if turn + 1 == len(turns):
                near_sum(leaf_len, bucket, first, first + count, lists_ref, left_ref,
                         src_ref.at[:emb], src_ref.at[emb:], out_ref)


def down_kernel(leaf_num, leaf_len, level_num, *refs):
    owns, couples = refs[:level_num], refs[level_num : 2 * level_num]
    tree_ref, tree_couple_ref, leaf_ref, near_ref, out_ref, field_ref = refs[2 * level_num :]
    skel_len = tree_ref.shape[1] // 2
    probe_num = out_ref.shape[0]

    def spread(field, high, low):
        field_high, field_low = halves(field)
        both = mm(jnp.concatenate([field_high, field_low], axis=0), high)
        return both[:probe_num] + both[probe_num:] + mm(field_high, low)

    field = jnp.zeros((probe_num, skel_len), F32)
    for own, couple in zip(reversed(owns), reversed(couples)):
        field = spread(field, own[:skel_len], own[skel_len:]) + couple[...]

    fields, row = [field], leaf_num - 2
    while len(fields) < leaf_num:
        below = []
        for k, field in enumerate(fields):
            both = spread(field, tree_ref[row + k, :skel_len, :],
                          tree_ref[row + k, skel_len:, :]) + tree_couple_ref[row + k]
            below += [both[:, :skel_len], both[:, skel_len:]]
        fields, row = below, row - len(below)
    for leaf, field in enumerate(fields):
        field_ref[leaf] = field

    for leaf in range(leaf_num):
        far = spread(field_ref[leaf], leaf_ref[leaf, :skel_len, :], leaf_ref[leaf, skel_len:, :])
        cols = slice(leaf * leaf_len, (leaf + 1) * leaf_len)
        out_ref[:, cols] = near_ref[:, cols] + far


def whole(num):
    return [pl.BlockSpec(memory_space=pltpu.VMEM)] * num


def params():
    return pltpu.CompilerParams(vmem_limit_bytes=VMEM_MIB * 1024 * 1024)


def cost(flops, read):
    return pl.CostEstimate(flops=flops, bytes_accessed=read, transcendentals=0)


def across_link(block, axis):
    count = lax.axis_size(axis)
    route = [(i, i + 1) for i in range(1, count - 1, 2)]
    return lax.ppermute(block, axis, route + [(j, i) for i, j in route])


def partner(block, axis, stride):
    count = lax.axis_size(axis)
    return lax.ppermute(block, axis, [(i, i ^ (1 << stride)) for i in range(count)])


def per_device(points, probes, near_list, near_count, leaf_skel, local_skel, upper_skel):
    emb, shard_len = points.shape
    leaf_num, slot_num = near_list.shape
    leaf_len = shard_len // leaf_num
    skel_len = leaf_skel.shape[1]
    probe_num = probes.shape[0]
    me = lax.axis_index("leaf")
    dev_num = lax.axis_size("leaf")
    level_num = dev_num.bit_length() - 1
    node_rows = emb + 2 * AUG + probe_num
    node_total = 2 * leaf_num - 1

    chip_span = leaf_num // CHIP_PARTS

    joined = jnp.concatenate([points, probes], axis=0)
    link = across_link(joined, "leaf")

    relative = near_list - (me * leaf_num - leaf_num)
    odd = (me & 1) == 1
    relative = jnp.where(
        odd & (relative < leaf_num), relative + 2 * leaf_num,
        jnp.where(odd & (relative >= 2 * leaf_num), relative - 2 * leaf_num, relative))
    bits = jnp.arange(level_num, dtype=jnp.int32)
    rows = dev_num - (dev_num >> bits) + (me >> (bits + 1))
    chosen = jnp.take(upper_skel, rows, axis=0) ^ (((me >> bits) & 1) * skel_len)[:, None]

    sd = jax.ShapeDtypeStruct
    cur, leaf_kern, tree, tree_couple, left = pl.pallas_call(
        functools.partial(up_kernel, emb, leaf_num, leaf_len, GROUP),
        out_shape=(
            sd((node_rows, skel_len), BF16),
            sd((leaf_num, 2 * skel_len, leaf_len), BF16),
            sd((leaf_num - 1, 2 * skel_len, 2 * skel_len), BF16),
            sd((leaf_num - 1, probe_num, 2 * skel_len), F32),
            sd((leaf_num, leaf_len, emb + AUG), BF16),
        ),
        in_specs=whole(3),
        out_specs=tuple(whole(5)),
        scratch_shapes=[pltpu.VMEM((node_total, node_rows, skel_len), BF16)],
        compiler_params=params(),
        cost_estimate=cost(5_000_000_000, 4_000_000),
        name="up",
    )(joined, leaf_skel, local_skel)

    bucket_num = 3 + CHIP_PARTS
    smem = [pl.BlockSpec(memory_space=pltpu.SMEM)]
    near, lists = pl.pallas_call(
        functools.partial(near_own_kernel, emb, leaf_len, chip_span),
        out_shape=(
            sd((probe_num, shard_len), F32),
            sd((2 * bucket_num + 1, leaf_num * slot_num), jnp.int32),
        ),
        in_specs=smem * 2 + whole(2),
        out_specs=tuple(whole(1) + smem),
        compiler_params=params(),
        cost_estimate=cost(5_000_000_000, 4_000_000),
        name="near_own",
    )(relative, near_count, left, joined)

    def near_call(near, turns, sources):
        return pl.pallas_call(
            functools.partial(near_kernel, emb, leaf_len, turns),
            out_shape=sd(near.shape, F32),
            in_specs=smem + whole(2 + len(sources)),
            out_specs=whole(1)[0],
            input_output_aliases={2 + len(sources): 0},
            compiler_params=params(),
            cost_estimate=cost(1_000_000_000, 1_000_000),
            name="near_beside",
        )(lists, left, *sources, near)

    chip_wide = chip_span * leaf_len
    parts = [joined[:, k * chip_wide : (k + 1) * chip_wide] for k in range(CHIP_PARTS)]
    cur, near, chosen, parts = lax.optimization_barrier((cur, near, chosen, parts))
    arrived, turns = {-1: link}, ()

    owns, couples = [], []
    for level in range(level_num):
        sib = partner(cur, "leaf", level)
        for k in SENDS.get(level, ()):
            part, cur = lax.optimization_barrier((parts[k], cur))
            arrived[k] = partner(part, "leaf", 0)
        if level in SUMS:
            budget, ks = SUMS[level]
            turns += ((budget, tuple(2 + k for k in ks)),)
            cur, near = lax.optimization_barrier((cur, near))
            near = near_call(near, turns, [arrived[k] for k in ks])
            sib, near = lax.optimization_barrier((sib, near))
        more = 1 if level + 1 < level_num else 0
        couple, own, *rest = pl.pallas_call(
            functools.partial(level_kernel, emb),
            out_shape=(
                sd((probe_num, skel_len), F32),
                sd((2 * skel_len, skel_len), BF16),
            ) + (sd((node_rows, skel_len), BF16),) * more,
            in_specs=whole(3),
            out_specs=tuple(whole(2 + more)),
            compiler_params=params(),
            cost_estimate=cost(1_000_000_000, 200_000),
            name="level",
        )(cur, sib, chosen[level : level + 1])
        if rest:
            cur = rest[0]
        owns.append(own)
        couples.append(couple)

    return pl.pallas_call(
        functools.partial(down_kernel, leaf_num, leaf_len, level_num),
        out_shape=sd((probe_num, shard_len), F32),
        in_specs=whole(2 * level_num + 4),
        out_specs=whole(1)[0],
        scratch_shapes=[pltpu.VMEM((leaf_num, probe_num, skel_len), F32)],
        compiler_params=params(),
        cost_estimate=cost(5_000_000_000, 4_000_000),
        name="down",
    )(*owns, *couples, tree, tree_couple, leaf_kern, near)


def solution(mesh):
    in_specs = (
        P(None, "leaf"),
        P(None, "leaf"),
        P("leaf", None),
        P("leaf"),
        P("leaf", None),
        P("leaf", None),
        P(),
    )
    return jax.shard_map(
        per_device, mesh=mesh, in_specs=in_specs, out_specs=P(None, "leaf"), check_vma=False
    )
```

profile of v0, /device:TPU:2, one launch (start us, length us, event | category | flops | bytes accessed | tf_op | source)
XLA Modules:
  0.0 81.8 jit_solution(1211559884362714976)
XLA Ops:
  0.0 0.0 copy-start
  0.0 0.0 copy-start.4
  0.0 0.0 copy-start.5
  0.0 0.0 copy-start.2
  0.0 0.0 copy-start.1
  0.0 3.2 %constant_dynamic-update-slice_fusion.1 = bf16[144,8192]{1,0:T(8,128)(2,1)} fusion(bf16[128,8192]{1,0:T(8,128)(2,1)} %param.7), kind=kLoop, calls=%fused_computation.5 | loop fusion | bytes 4194304
  3.2 0.0 copy-done.4
  3.2 0.7 constant_dynamic-update-slice_fusion.all_ref
  3.9 9.6 %collective-permute-start.3 = (bf16[144,8192]{1,0:T(8,128)(2,1)}, bf16[144,8192]{1,0:T(8,128)(2,1)S(1)}, u32[]{:S(2)}, u32[]{:S(2)}) collective-permute-start(bf16[144,8192]{1,0:T(8,128)(2,1)} %constant_dynamic-update-slice_fusion.all_ref), channel_id=1, source_target_pairs={{1,2},{3,4},{5,6},{7,8},{9,10},{11,12},{13,14},{15,16},{17,18},{19... | collective-permute-start | bytes 7077896 | tf_op jit(solution)/shard_map/ppermute | solution.py:299
  13.6 0.0 copy-done
  13.6 0.6 gather_fusion
  14.2 0.1 select_xor_fusion
  14.3 0.0 copy-done.5
  14.3 0.1 copy.14
  14.4 0.0 copy-done.2
  14.4 0.0 copy-done.1
  14.4 0.0 copy-start.3
  14.4 7.9 %up.1 = (bf16[176,128]{1,0:T(8,128)(2,1)S(1)}, bf16[16,256,512]{2,1,0:T(8,128)(2,1)S(1)}, bf16[15,256,256]{2,1,0:T(8,128)(2,1)S(1)}, f32[15,16,256]{2,1,0:T(8,128)S(1)}, bf16[16,512,144]{2,1,0:T(8,128)(2,1)S(1)}) custom-call(bf16[144,8192]{1,0:T(8,128)(2,1)} %constant_dynamic-update-slice_fusion.all_ref, s32[16,128]{1,0:T(8,128)S(1)} %copy-done.1, ...), custom_call_target="tpu_custom_call" | custom-call | flops 5000000000 | bytes 4000000 | tf_op jit(solution)/shard_map/up/pallas_call | solution.py:334
  22.3 0.0 copy-done.3
  22.3 11.1 %near_own.1 = (f32[16,8192]{1,0:T(8,128)S(1)}, s32[15,64]{1,0:T(8,128)S(1)}) custom-call(s32[16,4]{1,0:T(8,128)S(1)} %fusion.ids_ref, s32[16]{0:T(128)S(1)} %copy-done.3, bf16[16,512,144]{2,1,0:T(8,128)(2,1)S(1)} %get-tuple-element.75.left_ref, bf16[144,8192]{1,0:T(8,128)(2,1)} %constant_dynamic-update-slice_fusion.all_ref), custom_call_target="tpu_custom_call" | custom-call | flops 5000000000 | bytes 4000000 | tf_op jit(solution)/shard_map/near_own/pallas_call | solution.py:353
  33.4 1.8 %fusion.2 = (bf16[144,2048]{1,0:T(8,128)(2,1)S(1)}, bf16[144,2048]{1,0:T(8,128)(2,1)S(1)}, bf16[144,2048]{1,0:T(8,128)(2,1)S(1)}, bf16[144,2048]{1,0:T(8,128)(2,1)S(1)}) fusion(bf16[144,8192]{1,0:T(8,128)(2,1)} %constant_dynamic-update-slice_fusion.all_ref), kind=kLoop, calls=%fused_computation.12 | loop fusion | bytes 4718592 | tf_op jit(solution)/shard_map/slice | solution.py:379
  35.2 0.1 collective-permute-start
  35.3 1.2 %collective-permute-done.sib_ref = bf16[176,128]{1,0:T(8,128)(2,1)S(1)} collective-permute-done((bf16[176,128]{1,0:T(8,128)(2,1)S(1)}, bf16[176,128]{1,0:T(8,128)(2,1)S(1)}, u32[]{:S(2)}, u32[]{:S(2)}) %collective-permute-start) | collective-permute-done | bytes 45088 | tf_op jit(solution)/shard_map/ppermute | solution.py:304
  36.5 0.5 level.8
  37.1 0.0 collective-permute-start.1
  37.1 4.1 %collective-permute-done.1.sib_ref = bf16[176,128]{1,0:T(8,128)(2,1)S(1)} collective-permute-done((bf16[176,128]{1,0:T(8,128)(2,1)S(1)}, bf16[176,128]{1,0:T(8,128)(2,1)S(1)}, u32[]{:S(2)}, u32[]{:S(2)}) %collective-permute-start.1) | collective-permute-done | bytes 45088 | tf_op jit(solution)/shard_map/ppermute | solution.py:304
  41.2 0.5 level.9
  41.7 0.0 collective-permute-start.6
  41.7 0.1 collective-permute-start.2
  41.8 0.0 collective-permute-done.3.refs_0_
  41.8 1.6 %near_beside.6.refs_1_ = f32[16,8192]{1,0:T(8,128)S(1)} custom-call(s32[15,64]{1,0:T(8,128)S(1)} %get-tuple-element.87.lists_ref, bf16[16,512,144]{2,1,0:T(8,128)(2,1)S(1)} %get-tuple-element.75.left_ref, bf16[144,8192]{1,0:T(8,128)(2,1)S(1)} %collective-permute-done.3.refs_0_, f32[16,8192]{1,0:T(8,128)S(1)} %get-tuple-element.88.refs_1_), custom_call_target="tpu_custom_call", output_to_operand_aliasing={{}: (3, {})} | custom-call | flops 1000000000 | bytes 1000000 | tf_op jit(solution)/shard_map/near_beside/pallas_call | solution.py:367
  43.5 3.9 %collective-permute-done.2.sib_ref = bf16[176,128]{1,0:T(8,128)(2,1)S(1)} collective-permute-done((bf16[176,128]{1,0:T(8,128)(2,1)S(1)}, bf16[176,128]{1,0:T(8,128)(2,1)S(1)}, u32[]{:S(2)}, u32[]{:S(2)}) %collective-permute-start.2) | collective-permute-done | bytes 45088 | tf_op jit(solution)/shard_map/ppermute | solution.py:304
  47.4 0.5 level.10
  47.9 0.0 collective-permute-start.4
  47.9 0.1 collective-permute-start.8
  48.0 2.1 %near_beside.7.refs_2_ = f32[16,8192]{1,0:T(8,128)S(1)} custom-call(s32[15,64]{1,0:T(8,128)S(1)} %get-tuple-element.87.lists_ref, bf16[16,512,144]{2,1,0:T(8,128)(2,1)S(1)} %get-tuple-element.75.left_ref, bf16[144,8192]{1,0:T(8,128)(2,1)S(1)} %collective-permute-done.3.refs_0_, f32[16,8192]{1,0:T(8,128)S(1)} %near_beside.6.refs_1_), custom_call_target="tpu_custom_call", output_to_operand_aliasing={{}: (3, {})} | custom-call | flops 1000000000 | bytes 1000000 | tf_op jit(solution)/shard_map/near_beside/pallas_call | solution.py:367
  50.2 1.8 %collective-permute-done.4.sib_ref = bf16[176,128]{1,0:T(8,128)(2,1)S(1)} collective-permute-done((bf16[176,128]{1,0:T(8,128)(2,1)S(1)}, bf16[176,128]{1,0:T(8,128)(2,1)S(1)}, u32[]{:S(2)}, u32[]{:S(2)}) %collective-permute-start.4) | collective-permute-done | bytes 45088 | tf_op jit(solution)/shard_map/ppermute | solution.py:304
  52.0 0.5 level.11
  52.5 0.0 collective-permute-start.5
  52.6 0.1 collective-permute-start.10
  52.7 0.0 collective-permute-done.6.refs_1_
  52.7 2.6 %near_beside.8.refs_3_ = f32[16,8192]{1,0:T(8,128)S(1)} custom-call(s32[15,64]{1,0:T(8,128)S(1)} %get-tuple-element.87.lists_ref, bf16[16,512,144]{2,1,0:T(8,128)(2,1)S(1)} %get-tuple-element.75.left_ref, bf16[144,8192]{1,0:T(8,128)(2,1)S(1)} %collective-permute-done.3.refs_0_, ...), custom_call_target="tpu_custom_call", output_to_operand_aliasing={{}: (4, {})} | custom-call | flops 1000000000 | bytes 1000000 | tf_op jit(solution)/shard_map/near_beside/pallas_call | solution.py:367
  55.3 2.3 %collective-permute-done.5.sib_ref = bf16[176,128]{1,0:T(8,128)(2,1)S(1)} collective-permute-done((bf16[176,128]{1,0:T(8,128)(2,1)S(1)}, bf16[176,128]{1,0:T(8,128)(2,1)S(1)}, u32[]{:S(2)}, u32[]{:S(2)}) %collective-permute-start.5) | collective-permute-done | bytes 45088 | tf_op jit(solution)/shard_map/ppermute | solution.py:304
  57.6 0.5 level.12
  58.1 0.2 collective-permute-start.12
  58.3 2.5 %collective-permute-start.7 = (bf16[176,128]{1,0:T(8,128)(2,1)S(1)}, bf16[176,128]{1,0:T(8,128)(2,1)S(1)}, u32[]{:S(2)}, u32[]{:S(2)}) collective-permute-start(bf16[176,128]{1,0:T(8,128)(2,1)S(1)} %get-tuple-element.112.cur_ref), channel_id=1, source_target_pairs={{0,32},{1,33},{2,34},{3,35},{4,36},{5,37},{6,38},{7,39},{8,40},{9,... | collective-permute-start | bytes 135176 | tf_op jit(solution)/shard_map/ppermute | solution.py:304
  60.8 0.0 collective-permute-done.8.refs_2_
  60.8 6.5 %near_beside.9.refs_4_ = f32[16,8192]{1,0:T(8,128)S(1)} custom-call(s32[15,64]{1,0:T(8,128)S(1)} %get-tuple-element.87.lists_ref, bf16[16,512,144]{2,1,0:T(8,128)(2,1)S(1)} %get-tuple-element.75.left_ref, bf16[144,8192]{1,0:T(8,128)(2,1)S(1)} %collective-permute-done.3.refs_0_, ...), custom_call_target="tpu_custom_call", output_to_operand_aliasing={{}: (5, {})} | custom-call | flops 1000000000 | bytes 1000000 | tf_op jit(solution)/shard_map/near_beside/pallas_call | solution.py:367
  67.4 0.0 collective-permute-done.7.sib_ref
  67.4 0.6 level.13
  68.0 0.0 collective-permute-start.9
  68.0 0.0 collective-permute-done.10.refs_3_
  68.0 2.6 %near_beside.10.refs_5_ = f32[16,8192]{1,0:T(8,128)S(1)} custom-call(s32[15,64]{1,0:T(8,128)S(1)} %get-tuple-element.87.lists_ref, bf16[16,512,144]{2,1,0:T(8,128)(2,1)S(1)} %get-tuple-element.75.left_ref, bf16[144,8192]{1,0:T(8,128)(2,1)S(1)} %collective-permute-done.3.refs_0_, ...), custom_call_target="tpu_custom_call", output_to_operand_aliasing={{}: (6, {})} | custom-call | flops 1000000000 | bytes 1000000 | tf_op jit(solution)/shard_map/near_beside/pallas_call | solution.py:367
  70.6 1.4 %collective-permute-done.9.sib_ref = bf16[176,128]{1,0:T(8,128)(2,1)S(1)} collective-permute-done((bf16[176,128]{1,0:T(8,128)(2,1)S(1)}, bf16[176,128]{1,0:T(8,128)(2,1)S(1)}, u32[]{:S(2)}, u32[]{:S(2)}) %collective-permute-start.9) | collective-permute-done | bytes 45088 | tf_op jit(solution)/shard_map/ppermute | solution.py:304
  72.0 0.5 level.14
  72.6 1.4 %collective-permute-start.11 = (bf16[176,128]{1,0:T(8,128)(2,1)S(1)}, bf16[176,128]{1,0:T(8,128)(2,1)S(1)}, u32[]{:S(2)}, u32[]{:S(2)}) collective-permute-start(bf16[176,128]{1,0:T(8,128)(2,1)S(1)} %get-tuple-element.126.cur_ref), channel_id=1, source_target_pairs={{0,128},{1,129},{2,130},{3,131},{4,132},{5,133},{6,134},{7,135},{8... | collective-permute-start | bytes 135176 | tf_op jit(solution)/shard_map/ppermute | solution.py:304
  74.0 0.0 collective-permute-done.12.refs_4_
  74.0 3.1 %near_beside.11.refs_19_ = f32[16,8192]{1,0:T(8,128)S(1)} custom-call(s32[15,64]{1,0:T(8,128)S(1)} %get-tuple-element.87.lists_ref, bf16[16,512,144]{2,1,0:T(8,128)(2,1)S(1)} %get-tuple-element.75.left_ref, bf16[144,8192]{1,0:T(8,128)(2,1)S(1)} %collective-permute-done.3.refs_0_, ...), custom_call_target="tpu_custom_call", output_to_operand_aliasing={{}: (7, {})} | custom-call | flops 1000000000 | bytes 1000000 | tf_op jit(solution)/shard_map/near_beside/pallas_call | solution.py:367
  77.1 1.0 %collective-permute-done.11.sib_ref = bf16[176,128]{1,0:T(8,128)(2,1)S(1)} collective-permute-done((bf16[176,128]{1,0:T(8,128)(2,1)S(1)}, bf16[176,128]{1,0:T(8,128)(2,1)S(1)}, u32[]{:S(2)}, u32[]{:S(2)}) %collective-permute-start.11) | collective-permute-done | bytes 45088 | tf_op jit(solution)/shard_map/ppermute | solution.py:304
  78.2 0.6 level.15
  78.7 3.1 %down.1 = f32[16,8192]{1,0:T(8,128)} custom-call(bf16[256,128]{1,0:T(8,128)(2,1)S(1)} %get-tuple-element.79.refs_0_, bf16[256,128]{1,0:T(8,128)(2,1)S(1)} %get-tuple-element.81.refs_1_, bf16[256,128]{1,0:T(8,128)(2,1)S(1)} %get-tuple-element.90.refs_2_, bf16[256,128]{1,0:T(8,128)(2,1)S(1)} %get-tuple-element.98.refs_3_, ...), custom_call_target="tpu_custom_call" | custom-call | flops 5000000000 | bytes 4000000 | tf_op jit(solution)/shard_map/down/pallas_call | solution.py:413
  (6 shorter events, 0.0 us)
Async XLA Ops:
  0.0 13.6 %copy-start = (s32[255,128]{1,0:T(8,128)S(1)}, s32[255,128]{1,0:T(8,128)}, u32[]{:S(2)}) copy-start(s32[255,128]{1,0:T(8,128)} %param.13) | copy-start | bytes 391684
  0.0 3.2 %copy-start.4 = (bf16[16,8192]{1,0:T(8,128)(2,1)S(1)}, bf16[16,8192]{1,0:T(8,128)(2,1)}, u32[]{:S(2)}) copy-start(bf16[16,8192]{1,0:T(8,128)(2,1)} %param.8) | copy-start | bytes 786436
  0.0 14.3 %copy-start.5 = (s32[16,4]{0,1:T(4,128)S(1)}, s32[16,4]{0,1:T(4,128)}, u32[]{:S(2)}) copy-start(s32[16,4]{0,1:T(4,128)} %param.9) | copy-start | bytes 772
  0.0 14.4 %copy-start.2 = (s32[15,128]{1,0:T(8,128)S(1)}, s32[15,128]{1,0:T(8,128)}, u32[]{:S(2)}) copy-start(s32[15,128]{1,0:T(8,128)} %local_skel_ref.1) | copy-start | bytes 23044
  0.0 14.3 %copy-start.1 = (s32[16,128]{1,0:T(8,128)S(1)}, s32[16,128]{1,0:T(8,128)}, u32[]{:S(2)}) copy-start(s32[16,128]{1,0:T(8,128)} %leaf_skel_ref.1) | copy-start | bytes 24580
  3.9 37.9 %collective-permute-start.3 = (bf16[144,8192]{1,0:T(8,128)(2,1)}, bf16[144,8192]{1,0:T(8,128)(2,1)S(1)}, u32[]{:S(2)}, u32[]{:S(2)}) collective-permute-start(bf16[144,8192]{1,0:T(8,128)(2,1)} %constant_dynamic-update-slice_fusion.all_ref), channel_id=1, source_target_pairs={{1,2},{3,4},{5,6},{7,8},{9,10},{11,12},{13,14},{15,16},{17,18},{19... | collective-permute-start | bytes 7077896 | tf_op jit(solution)/shard_map/ppermute | solution.py:299
  14.4 7.9 %copy-start.3 = (s32[16]{0:T(128)S(1)}, s32[16]{0:T(128)}, u32[]{:S(2)}) copy-start(s32[16]{0:T(128)} %count_ref.1) | copy-start | bytes 196
  35.2 1.3 %collective-permute-start = (bf16[176,128]{1,0:T(8,128)(2,1)S(1)}, bf16[176,128]{1,0:T(8,128)(2,1)S(1)}, u32[]{:S(2)}, u32[]{:S(2)}) collective-permute-start(bf16[176,128]{1,0:T(8,128)(2,1)S(1)} %get-tuple-element.77.cur_ref), channel_id=1, source_target_pairs={{0,1},{1,0},{2,3},{3,2},{4,5},{5,4},{6,7},{7,6},{8,9},{9,8},{10,11... | collective-permute-start | bytes 135176 | tf_op jit(solution)/shard_map/ppermute | solution.py:304
  37.1 4.1 %collective-permute-start.1 = (bf16[176,128]{1,0:T(8,128)(2,1)S(1)}, bf16[176,128]{1,0:T(8,128)(2,1)S(1)}, u32[]{:S(2)}, u32[]{:S(2)}) collective-permute-start(bf16[176,128]{1,0:T(8,128)(2,1)S(1)} %get-tuple-element.80.cur_ref), channel_id=1, source_target_pairs={{0,2},{1,3},{2,0},{3,1},{4,6},{5,7},{6,4},{7,5},{8,10},{9,11},{10,... | collective-permute-start | bytes 135176 | tf_op jit(solution)/shard_map/ppermute | solution.py:304
  41.7 11.0 %collective-permute-start.6 = (bf16[144,2048]{1,0:T(8,128)(2,1)S(1)}, bf16[144,2048]{1,0:T(8,128)(2,1)S(1)}, u32[]{:S(2)}, u32[]{:S(2)}) collective-permute-start(bf16[144,2048]{1,0:T(8,128)(2,1)S(1)} %get-tuple-element.104), channel_id=1, source_target_pairs={{0,1},{1,0},{2,3},{3,2},{4,5},{5,4},{6,7},{7,6},{8,9},{9,8},{10,11... | collective-permute-start | bytes 1769480 | tf_op jit(solution)/shard_map/ppermute | solution.py:304
  41.7 5.6 %collective-permute-start.2 = (bf16[176,128]{1,0:T(8,128)(2,1)S(1)}, bf16[176,128]{1,0:T(8,128)(2,1)S(1)}, u32[]{:S(2)}, u32[]{:S(2)}) collective-permute-start(bf16[176,128]{1,0:T(8,128)(2,1)S(1)} %get-tuple-element.86.cur_ref), channel_id=1, source_target_pairs={{0,4},{1,5},{2,6},{3,7},{4,0},{5,1},{6,2},{7,3},{8,12},{9,13},{10,... | collective-permute-start | bytes 135176 | tf_op jit(solution)/shard_map/ppermute | solution.py:304
  47.9 4.1 %collective-permute-start.4 = (bf16[176,128]{1,0:T(8,128)(2,1)S(1)}, bf16[176,128]{1,0:T(8,128)(2,1)S(1)}, u32[]{:S(2)}, u32[]{:S(2)}) collective-permute-start(bf16[176,128]{1,0:T(8,128)(2,1)S(1)} %get-tuple-element.95.cur_ref), channel_id=1, source_target_pairs={{0,8},{1,9},{2,10},{3,11},{4,12},{5,13},{6,14},{7,15},{8,0},{9,1},... | collective-permute-start | bytes 135176 | tf_op jit(solution)/shard_map/ppermute | solution.py:304
  47.9 12.9 %collective-permute-start.8 = (bf16[144,2048]{1,0:T(8,128)(2,1)S(1)}, bf16[144,2048]{1,0:T(8,128)(2,1)S(1)}, u32[]{:S(2)}, u32[]{:S(2)}) collective-permute-start(bf16[144,2048]{1,0:T(8,128)(2,1)S(1)} %get-tuple-element.113), channel_id=1, source_target_pairs={{0,1},{1,0},{2,3},{3,2},{4,5},{5,4},{6,7},{7,6},{8,9},{9,8},{10,11... | collective-permute-start | bytes 1769480 | tf_op jit(solution)/shard_map/ppermute | solution.py:304
  52.5 5.1 %collective-permute-start.5 = (bf16[176,128]{1,0:T(8,128)(2,1)S(1)}, bf16[176,128]{1,0:T(8,128)(2,1)S(1)}, u32[]{:S(2)}, u32[]{:S(2)}) collective-permute-start(bf16[176,128]{1,0:T(8,128)(2,1)S(1)} %get-tuple-element.103.cur_ref), channel_id=1, source_target_pairs={{0,16},{1,17},{2,18},{3,19},{4,20},{5,21},{6,22},{7,23},{8,24},{9,... | collective-permute-start | bytes 135176 | tf_op jit(solution)/shard_map/ppermute | solution.py:304
  52.6 15.4 %collective-permute-start.10 = (bf16[144,2048]{1,0:T(8,128)(2,1)S(1)}, bf16[144,2048]{1,0:T(8,128)(2,1)S(1)}, u32[]{:S(2)}, u32[]{:S(2)}) collective-permute-start(bf16[144,2048]{1,0:T(8,128)(2,1)S(1)} %get-tuple-element.120), channel_id=1, source_target_pairs={{0,1},{1,0},{2,3},{3,2},{4,5},{5,4},{6,7},{7,6},{8,9},{9,8},{10,11... | collective-permute-start | bytes 1769480 | tf_op jit(solution)/shard_map/ppermute | solution.py:304
  58.1 15.9 %collective-permute-start.12 = (bf16[144,2048]{1,0:T(8,128)(2,1)S(1)}, bf16[144,2048]{1,0:T(8,128)(2,1)S(1)}, u32[]{:S(2)}, u32[]{:S(2)}) collective-permute-start(bf16[144,2048]{1,0:T(8,128)(2,1)S(1)} %get-tuple-element.127), channel_id=1, source_target_pairs={{0,1},{1,0},{2,3},{3,2},{4,5},{5,4},{6,7},{7,6},{8,9},{9,8},{10,11... | collective-permute-start | bytes 1769480 | tf_op jit(solution)/shard_map/ppermute | solution.py:304
  58.3 9.0 %collective-permute-start.7 = (bf16[176,128]{1,0:T(8,128)(2,1)S(1)}, bf16[176,128]{1,0:T(8,128)(2,1)S(1)}, u32[]{:S(2)}, u32[]{:S(2)}) collective-permute-start(bf16[176,128]{1,0:T(8,128)(2,1)S(1)} %get-tuple-element.112.cur_ref), channel_id=1, source_target_pairs={{0,32},{1,33},{2,34},{3,35},{4,36},{5,37},{6,38},{7,39},{8,40},{9,... | collective-permute-start | bytes 135176 | tf_op jit(solution)/shard_map/ppermute | solution.py:304
  68.0 4.1 %collective-permute-start.9 = (bf16[176,128]{1,0:T(8,128)(2,1)S(1)}, bf16[176,128]{1,0:T(8,128)(2,1)S(1)}, u32[]{:S(2)}, u32[]{:S(2)}) collective-permute-start(bf16[176,128]{1,0:T(8,128)(2,1)S(1)} %get-tuple-element.119.cur_ref), channel_id=1, source_target_pairs={{0,64},{1,65},{2,66},{3,67},{4,68},{5,69},{6,70},{7,71},{8,72},{9,... | collective-permute-start | bytes 135176 | tf_op jit(solution)/shard_map/ppermute | solution.py:304
  72.6 5.6 %collective-permute-start.11 = (bf16[176,128]{1,0:T(8,128)(2,1)S(1)}, bf16[176,128]{1,0:T(8,128)(2,1)S(1)}, u32[]{:S(2)}, u32[]{:S(2)}) collective-permute-start(bf16[176,128]{1,0:T(8,128)(2,1)S(1)} %get-tuple-element.126.cur_ref), channel_id=1, source_target_pairs={{0,128},{1,129},{2,130},{3,131},{4,132},{5,133},{6,134},{7,135},{8... | collective-permute-start | bytes 135176 | tf_op jit(solution)/shard_map/ppermute | solution.py:304
where the time goes:
time: 82 us; the launch traced here: 81.8 us
  Pallas kernels  45 us (55%)
  waiting for transfers between devices  15.8 us (19%)
  starting transfers between devices  14.3 us (17%)
  local copies, waits for them, and re-layouts  6.36 us (8%)
    pallas_call x6, Pallas kernels, near_call(): pl.pallas_call(functools.partial(near_kernel, emb, leaf_len, turns), out_...  18.7 us
    ppermute x12, waiting for transfers between devices, partner(): lax.ppermute(block, axis, [(i, i ^ 1 << stride) for i in range(count)])  15.8 us
    pallas_call x1, Pallas kernels, per_device(): pl.pallas_call(functools.partial(near_own_kernel, emb, leaf_len, chip_spa...  11.1 us
    ppermute x1, starting transfers between devices, across_link(): return lax.ppermute(block, axis, route + [(j, i) for i, j in route])  9.61 us
    pallas_call x1, Pallas kernels, per_device(): pl.pallas_call(functools.partial(up_kernel, emb, leaf_num, leaf_len, GROU...  7.91 us
    ppermute x12, starting transfers between devices, partner(): lax.ppermute(block, axis, [(i, i ^ 1 << stride) for i in range(count)])  4.69 us
    pallas_call x8, Pallas kernels, per_device(): pl.pallas_call(functools.partial(level_kernel, emb), out_shape=(sd((probe...  4.25 us
    unnamed x14, local copies, waits for them, and re-layouts  3.29 us
  transfers between devices with their start and end apart: 13, of which 7 were waited for; matrix products, arithmetic and copies ran while one was open for 3% of the time, Pallas kernels for 51%

commit v1 on v0

--- a/solution.py
+++ b/solution.py
@@ -17,13 +17,13 @@
 GROUP = 8
 NEAR_TILE = 512
 CHIP_PARTS = 4
-SENDS = {2: (0,), 3: (1,), 4: (2,), 5: (3,)}
+SENDS = {1: (0,), 2: (1,), 3: (2,), 4: (3,)}
 SUMS = {
     2: (2, (-1,)),
-    3: (3, (-1,)),
-    4: (4, (-1, 0)),
-    5: (12, (-1, 0, 1)),
-    6: (4, (-1, 0, 1, 2)),
+    3: (3, (-1, 0)),
+    4: (4, (-1, 0, 1)),
+    5: (12, (-1, 0, 1, 2)),
+    6: (4, (-1, 0, 1, 2, 3)),
     7: (None, (-1, 0, 1, 2, 3)),
 }
 

time: 82 us -> 83.3 us (1.016)
  waiting for transfers between devices: 15.8 us -> 17 us
    ppermute x12, waiting for transfers between devices: 15.8 us -> 17 us  [partner(): lax.ppermute(block, axis, [(i, i ^ 1 << stride) for i in range(count)])]
  transfers between devices with their start and end apart: 13 -> 13, of which waited for: 7 -> 7; matrix products, arithmetic and copies ran while one was open for 3% -> 3% of each run, Pallas kernels for 51% -> 49%
where the time goes in v1:
time: 83.3 us; the launch traced here: 83.1 us
  Pallas kernels  45.1 us (54%)
  waiting for transfers between devices  17 us (20%)
  starting transfers between devices  14.3 us (17%)
  local copies, waits for them, and re-layouts  6.36 us (8%)
    pallas_call x6, Pallas kernels, near_call(): pl.pallas_call(functools.partial(near_kernel, emb, leaf_len, turns), out_...  18.8 us
    ppermute x12, waiting for transfers between devices, partner(): lax.ppermute(block, axis, [(i, i ^ 1 << stride) for i in range(count)])  17 us
    pallas_call x1, Pallas kernels, per_device(): pl.pallas_call(functools.partial(near_own_kernel, emb, leaf_len, chip_spa...  11.1 us
    ppermute x1, starting transfers between devices, across_link(): return lax.ppermute(block, axis, route + [(j, i) for i, j in route])  9.61 us
    pallas_call x1, Pallas kernels, per_device(): pl.pallas_call(functools.partial(up_kernel, emb, leaf_num, leaf_len, GROU...  7.9 us
    ppermute x12, starting transfers between devices, partner(): lax.ppermute(block, axis, [(i, i ^ 1 << stride) for i in range(count)])  4.65 us
    pallas_call x8, Pallas kernels, per_device(): pl.pallas_call(functools.partial(level_kernel, emb), out_shape=(sd((probe...  4.25 us
    unnamed x14, local copies, waits for them, and re-layouts  3.28 us
  transfers between devices with their start and end apart: 13, of which 7 were waited for; matrix products, arithmetic and copies ran while one was open for 3% of the time, Pallas kernels for 49%

profile of v1, /device:TPU:2, one launch (start us, length us, event | category | flops | bytes accessed | tf_op | source)
XLA Modules:
  0.0 83.1 jit_solution(15042582649587391345)
XLA Ops:
  0.0 0.0 copy-start
  0.0 0.0 copy-start.4
  0.0 0.0 copy-start.5
  0.0 0.0 copy-start.2
  0.0 0.0 copy-start.1
  0.0 3.2 %constant_dynamic-update-slice_fusion.1 = bf16[144,8192]{1,0:T(8,128)(2,1)} fusion(bf16[128,8192]{1,0:T(8,128)(2,1)} %param.7), kind=kLoop, calls=%fused_computation.5 | loop fusion | bytes 4194304
  3.2 0.0 copy-done.4
  3.2 0.7 constant_dynamic-update-slice_fusion.all_ref
  3.9 9.6 %collective-permute-start.3 = (bf16[144,8192]{1,0:T(8,128)(2,1)}, bf16[144,8192]{1,0:T(8,128)(2,1)S(1)}, u32[]{:S(2)}, u32[]{:S(2)}) collective-permute-start(bf16[144,8192]{1,0:T(8,128)(2,1)} %constant_dynamic-update-slice_fusion.all_ref), channel_id=1, source_target_pairs={{1,2},{3,4},{5,6},{7,8},{9,10},{11,12},{13,14},{15,16},{17,18},{19... | collective-permute-start | bytes 7077896 | tf_op jit(solution)/shard_map/ppermute | solution.py:299
  13.6 0.0 copy-done.5
  13.6 0.1 copy.14
  13.7 0.0 copy-done
  13.7 0.6 gather_fusion
  14.3 0.1 select_xor_fusion
  14.4 0.0 copy-done.2
  14.4 0.0 copy-done.1
  14.4 0.0 copy-start.3
  14.4 7.9 %up.1 = (bf16[176,128]{1,0:T(8,128)(2,1)S(1)}, bf16[16,256,512]{2,1,0:T(8,128)(2,1)S(1)}, bf16[15,256,256]{2,1,0:T(8,128)(2,1)S(1)}, f32[15,16,256]{2,1,0:T(8,128)S(1)}, bf16[16,512,144]{2,1,0:T(8,128)(2,1)S(1)}) custom-call(bf16[144,8192]{1,0:T(8,128)(2,1)} %constant_dynamic-update-slice_fusion.all_ref, s32[16,128]{1,0:T(8,128)S(1)} %copy-done.1, ...), custom_call_target="tpu_custom_call" | custom-call | flops 5000000000 | bytes 4000000 | tf_op jit(solution)/shard_map/up/pallas_call | solution.py:334
  22.3 0.0 copy-done.3
  22.3 11.1 %near_own.1 = (f32[16,8192]{1,0:T(8,128)S(1)}, s32[15,64]{1,0:T(8,128)S(1)}) custom-call(s32[16,4]{1,0:T(8,128)S(1)} %fusion.ids_ref, s32[16]{0:T(128)S(1)} %copy-done.3, bf16[16,512,144]{2,1,0:T(8,128)(2,1)S(1)} %get-tuple-element.75.left_ref, bf16[144,8192]{1,0:T(8,128)(2,1)} %constant_dynamic-update-slice_fusion.all_ref), custom_call_target="tpu_custom_call" | custom-call | flops 5000000000 | bytes 4000000 | tf_op jit(solution)/shard_map/near_own/pallas_call | solution.py:353
  33.4 1.8 %fusion.2 = (bf16[144,2048]{1,0:T(8,128)(2,1)S(1)}, bf16[144,2048]{1,0:T(8,128)(2,1)S(1)}, bf16[144,2048]{1,0:T(8,128)(2,1)S(1)}, bf16[144,2048]{1,0:T(8,128)(2,1)S(1)}) fusion(bf16[144,8192]{1,0:T(8,128)(2,1)} %constant_dynamic-update-slice_fusion.all_ref), kind=kLoop, calls=%fused_computation.12 | loop fusion | bytes 4718592 | tf_op jit(solution)/shard_map/slice | solution.py:379
  35.2 0.1 collective-permute-start
  35.3 1.2 %collective-permute-done.sib_ref = bf16[176,128]{1,0:T(8,128)(2,1)S(1)} collective-permute-done((bf16[176,128]{1,0:T(8,128)(2,1)S(1)}, bf16[176,128]{1,0:T(8,128)(2,1)S(1)}, u32[]{:S(2)}, u32[]{:S(2)}) %collective-permute-start) | collective-permute-done | bytes 45088 | tf_op jit(solution)/shard_map/ppermute | solution.py:304
  36.5 0.5 level.8
  37.0 0.2 collective-permute-start.5
  37.2 0.0 collective-permute-start.1
  37.2 4.0 %collective-permute-done.1.sib_ref = bf16[176,128]{1,0:T(8,128)(2,1)S(1)} collective-permute-done((bf16[176,128]{1,0:T(8,128)(2,1)S(1)}, bf16[176,128]{1,0:T(8,128)(2,1)S(1)}, u32[]{:S(2)}, u32[]{:S(2)}) %collective-permute-start.1) | collective-permute-done | bytes 45088 | tf_op jit(solution)/shard_map/ppermute | solution.py:304
  41.3 0.5 level.9
  41.8 0.0 collective-permute-start.2
  41.9 0.1 collective-permute-start.7
  42.0 0.0 collective-permute-done.3.refs_0_
  42.0 1.6 %near_beside.6.refs_2_ = f32[16,8192]{1,0:T(8,128)S(1)} custom-call(s32[15,64]{1,0:T(8,128)S(1)} %get-tuple-element.89.lists_ref, bf16[16,512,144]{2,1,0:T(8,128)(2,1)S(1)} %get-tuple-element.75.left_ref, bf16[144,8192]{1,0:T(8,128)(2,1)S(1)} %collective-permute-done.3.refs_0_, f32[16,8192]{1,0:T(8,128)S(1)} %get-tuple-element.90.refs_1_), custom_call_target="tpu_custom_call", output_to_operand_aliasing={{}: (3, {})} | custom-call | flops 1000000000 | bytes 1000000 | tf_op jit(solution)/shard_map/near_beside/pallas_call | solution.py:367
  43.6 3.8 %collective-permute-done.2.sib_ref = bf16[176,128]{1,0:T(8,128)(2,1)S(1)} collective-permute-done((bf16[176,128]{1,0:T(8,128)(2,1)S(1)}, bf16[176,128]{1,0:T(8,128)(2,1)S(1)}, u32[]{:S(2)}, u32[]{:S(2)}) %collective-permute-start.2) | collective-permute-done | bytes 45088 | tf_op jit(solution)/shard_map/ppermute | solution.py:304
  47.4 0.5 level.10
  47.9 0.0 collective-permute-start.4
  48.0 0.1 collective-permute-start.9
  48.1 0.0 collective-permute-done.5.refs_1_
  48.1 2.1 %near_beside.7.refs_3_ = f32[16,8192]{1,0:T(8,128)S(1)} custom-call(s32[15,64]{1,0:T(8,128)S(1)} %get-tuple-element.89.lists_ref, bf16[16,512,144]{2,1,0:T(8,128)(2,1)S(1)} %get-tuple-element.75.left_ref, bf16[144,8192]{1,0:T(8,128)(2,1)S(1)} %collective-permute-done.3.refs_0_, ...), custom_call_target="tpu_custom_call", output_to_operand_aliasing={{}: (4, {})} | custom-call | flops 1000000000 | bytes 1000000 | tf_op jit(solution)/shard_map/near_beside/pallas_call | solution.py:367
  50.2 1.8 %collective-permute-done.4.sib_ref = bf16[176,128]{1,0:T(8,128)(2,1)S(1)} collective-permute-done((bf16[176,128]{1,0:T(8,128)(2,1)S(1)}, bf16[176,128]{1,0:T(8,128)(2,1)S(1)}, u32[]{:S(2)}, u32[]{:S(2)}) %collective-permute-start.4) | collective-permute-done | bytes 45088 | tf_op jit(solution)/shard_map/ppermute | solution.py:304
  52.0 0.5 level.11
  52.6 0.0 collective-permute-start.11
  52.6 0.1 collective-permute-start.6
  52.7 0.0 collective-permute-done.7.refs_2_
  52.7 2.7 %near_beside.8.refs_4_ = f32[16,8192]{1,0:T(8,128)S(1)} custom-call(s32[15,64]{1,0:T(8,128)S(1)} %get-tuple-element.89.lists_ref, bf16[16,512,144]{2,1,0:T(8,128)(2,1)S(1)} %get-tuple-element.75.left_ref, bf16[144,8192]{1,0:T(8,128)(2,1)S(1)} %collective-permute-done.3.refs_0_, ...), custom_call_target="tpu_custom_call", output_to_operand_aliasing={{}: (5, {})} | custom-call | flops 1000000000 | bytes 1000000 | tf_op jit(solution)/shard_map/near_beside/pallas_call | solution.py:367
  55.5 2.7 %collective-permute-done.6.sib_ref = bf16[176,128]{1,0:T(8,128)(2,1)S(1)} collective-permute-done((bf16[176,128]{1,0:T(8,128)(2,1)S(1)}, bf16[176,128]{1,0:T(8,128)(2,1)S(1)}, u32[]{:S(2)}, u32[]{:S(2)}) %collective-permute-start.6) | collective-permute-done | bytes 45088 | tf_op jit(solution)/shard_map/ppermute | solution.py:304
  58.2 0.5 level.12
  58.7 3.4 %collective-permute-start.8 = (bf16[176,128]{1,0:T(8,128)(2,1)S(1)}, bf16[176,128]{1,0:T(8,128)(2,1)S(1)}, u32[]{:S(2)}, u32[]{:S(2)}) collective-permute-start(bf16[176,128]{1,0:T(8,128)(2,1)S(1)} %get-tuple-element.113.cur_ref), channel_id=1, source_target_pairs={{0,32},{1,33},{2,34},{3,35},{4,36},{5,37},{6,38},{7,39},{8,40},{9,... | collective-permute-start | bytes 135176 | tf_op jit(solution)/shard_map/ppermute | solution.py:304
  62.1 0.0 collective-permute-done.9.refs_3_
  62.1 6.5 %near_beside.9.refs_5_ = f32[16,8192]{1,0:T(8,128)S(1)} custom-call(s32[15,64]{1,0:T(8,128)S(1)} %get-tuple-element.89.lists_ref, bf16[16,512,144]{2,1,0:T(8,128)(2,1)S(1)} %get-tuple-element.75.left_ref, bf16[144,8192]{1,0:T(8,128)(2,1)S(1)} %collective-permute-done.3.refs_0_, ...), custom_call_target="tpu_custom_call", output_to_operand_aliasing={{}: (6, {})} | custom-call | flops 1000000000 | bytes 1000000 | tf_op jit(solution)/shard_map/near_beside/pallas_call | solution.py:367
  68.7 0.0 collective-permute-done.8.sib_ref
  68.7 0.6 level.13
  69.2 0.0 collective-permute-start.10
  69.3 0.0 collective-permute-done.11.refs_4_
  69.3 2.6 %near_beside.10.refs_5_ = f32[16,8192]{1,0:T(8,128)S(1)} custom-call(s32[15,64]{1,0:T(8,128)S(1)} %get-tuple-element.89.lists_ref, bf16[16,512,144]{2,1,0:T(8,128)(2,1)S(1)} %get-tuple-element.75.left_ref, bf16[144,8192]{1,0:T(8,128)(2,1)S(1)} %collective-permute-done.3.refs_0_, ...), custom_call_target="tpu_custom_call", output_to_operand_aliasing={{}: (7, {})} | custom-call | flops 1000000000 | bytes 1000000 | tf_op jit(solution)/shard_map/near_beside/pallas_call | solution.py:367
  71.9 1.4 %collective-permute-done.10.sib_ref = bf16[176,128]{1,0:T(8,128)(2,1)S(1)} collective-permute-done((bf16[176,128]{1,0:T(8,128)(2,1)S(1)}, bf16[176,128]{1,0:T(8,128)(2,1)S(1)}, u32[]{:S(2)}, u32[]{:S(2)}) %collective-permute-start.10) | collective-permute-done | bytes 45088 | tf_op jit(solution)/shard_map/ppermute | solution.py:304
  73.3 0.5 level.14
  73.9 0.5 collective-permute-start.12
  74.4 3.1 %near_beside.11.refs_19_ = f32[16,8192]{1,0:T(8,128)S(1)} custom-call(s32[15,64]{1,0:T(8,128)S(1)} %get-tuple-element.89.lists_ref, bf16[16,512,144]{2,1,0:T(8,128)(2,1)S(1)} %get-tuple-element.75.left_ref, bf16[144,8192]{1,0:T(8,128)(2,1)S(1)} %collective-permute-done.3.refs_0_, ...), custom_call_target="tpu_custom_call", output_to_operand_aliasing={{}: (7, {})} | custom-call | flops 1000000000 | bytes 1000000 | tf_op jit(solution)/shard_map/near_beside/pallas_call | solution.py:367
  77.5 2.0 %collective-permute-done.12.sib_ref = bf16[176,128]{1,0:T(8,128)(2,1)S(1)} collective-permute-done((bf16[176,128]{1,0:T(8,128)(2,1)S(1)}, bf16[176,128]{1,0:T(8,128)(2,1)S(1)}, u32[]{:S(2)}, u32[]{:S(2)}) %collective-permute-start.12) | collective-permute-done | bytes 45088 | tf_op jit(solution)/shard_map/ppermute | solution.py:304
  79.5 0.6 level.15
  80.0 3.1 %down.1 = f32[16,8192]{1,0:T(8,128)} custom-call(bf16[256,128]{1,0:T(8,128)(2,1)S(1)} %get-tuple-element.79.refs_0_, bf16[256,128]{1,0:T(8,128)(2,1)S(1)} %get-tuple-element.83.refs_1_, bf16[256,128]{1,0:T(8,128)(2,1)S(1)} %get-tuple-element.92.refs_2_, bf16[256,128]{1,0:T(8,128)(2,1)S(1)} %get-tuple-element.101.refs_3_, ...), custom_call_target="tpu_custom_call" | custom-call | flops 5000000000 | bytes 4000000 | tf_op jit(solution)/shard_map/down/pallas_call | solution.py:413
  (6 shorter events, 0.1 us)
Async XLA Ops:
  0.0 13.7 %copy-start = (s32[255,128]{1,0:T(8,128)S(1)}, s32[255,128]{1,0:T(8,128)}, u32[]{:S(2)}) copy-start(s32[255,128]{1,0:T(8,128)} %param.13) | copy-start | bytes 391684
  0.0 3.2 %copy-start.4 = (bf16[16,8192]{1,0:T(8,128)(2,1)S(1)}, bf16[16,8192]{1,0:T(8,128)(2,1)}, u32[]{:S(2)}) copy-start(bf16[16,8192]{1,0:T(8,128)(2,1)} %param.8) | copy-start | bytes 786436
  0.0 13.6 %copy-start.5 = (s32[16,4]{0,1:T(4,128)S(1)}, s32[16,4]{0,1:T(4,128)}, u32[]{:S(2)}) copy-start(s32[16,4]{0,1:T(4,128)} %param.9) | copy-start | bytes 772
  0.0 14.4 %copy-start.2 = (s32[15,128]{1,0:T(8,128)S(1)}, s32[15,128]{1,0:T(8,128)}, u32[]{:S(2)}) copy-start(s32[15,128]{1,0:T(8,128)} %local_skel_ref.1) | copy-start | bytes 23044
  0.0 14.3 %copy-start.1 = (s32[16,128]{1,0:T(8,128)S(1)}, s32[16,128]{1,0:T(8,128)}, u32[]{:S(2)}) copy-start(s32[16,128]{1,0:T(8,128)} %leaf_skel_ref.1) | copy-start | bytes 24580
  3.9 38.0 %collective-permute-start.3 = (bf16[144,8192]{1,0:T(8,128)(2,1)}, bf16[144,8192]{1,0:T(8,128)(2,1)S(1)}, u32[]{:S(2)}, u32[]{:S(2)}) collective-permute-start(bf16[144,8192]{1,0:T(8,128)(2,1)} %constant_dynamic-update-slice_fusion.all_ref), channel_id=1, source_target_pairs={{1,2},{3,4},{5,6},{7,8},{9,10},{11,12},{13,14},{15,16},{17,18},{19... | collective-permute-start | bytes 7077896 | tf_op jit(solution)/shard_map/ppermute | solution.py:299
  14.4 7.9 %copy-start.3 = (s32[16]{0:T(128)S(1)}, s32[16]{0:T(128)}, u32[]{:S(2)}) copy-start(s32[16]{0:T(128)} %count_ref.1) | copy-start | bytes 196
  35.2 1.3 %collective-permute-start = (bf16[176,128]{1,0:T(8,128)(2,1)S(1)}, bf16[176,128]{1,0:T(8,128)(2,1)S(1)}, u32[]{:S(2)}, u32[]{:S(2)}) collective-permute-start(bf16[176,128]{1,0:T(8,128)(2,1)S(1)} %get-tuple-element.77.cur_ref), channel_id=1, source_target_pairs={{0,1},{1,0},{2,3},{3,2},{4,5},{5,4},{6,7},{7,6},{8,9},{9,8},{10,11... | collective-permute-start | bytes 135176 | tf_op jit(solution)/shard_map/ppermute | solution.py:304
  37.0 11.1 %collective-permute-start.5 = (bf16[144,2048]{1,0:T(8,128)(2,1)S(1)}, bf16[144,2048]{1,0:T(8,128)(2,1)S(1)}, u32[]{:S(2)}, u32[]{:S(2)}) collective-permute-start(bf16[144,2048]{1,0:T(8,128)(2,1)S(1)} %get-tuple-element.98), channel_id=1, source_target_pairs={{0,1},{1,0},{2,3},{3,2},{4,5},{5,4},{6,7},{7,6},{8,9},{9,8},{10,11... | collective-permute-start | bytes 1769480 | tf_op jit(solution)/shard_map/ppermute | solution.py:304
  37.2 4.0 %collective-permute-start.1 = (bf16[176,128]{1,0:T(8,128)(2,1)S(1)}, bf16[176,128]{1,0:T(8,128)(2,1)S(1)}, u32[]{:S(2)}, u32[]{:S(2)}) collective-permute-start(bf16[176,128]{1,0:T(8,128)(2,1)S(1)} %get-tuple-element.82.cur_ref), channel_id=1, source_target_pairs={{0,2},{1,3},{2,0},{3,1},{4,6},{5,7},{6,4},{7,5},{8,10},{9,11},{10,... | collective-permute-start | bytes 135176 | tf_op jit(solution)/shard_map/ppermute | solution.py:304
  41.8 5.6 %collective-permute-start.2 = (bf16[176,128]{1,0:T(8,128)(2,1)S(1)}, bf16[176,128]{1,0:T(8,128)(2,1)S(1)}, u32[]{:S(2)}, u32[]{:S(2)}) collective-permute-start(bf16[176,128]{1,0:T(8,128)(2,1)S(1)} %get-tuple-element.88.cur_ref), channel_id=1, source_target_pairs={{0,4},{1,5},{2,6},{3,7},{4,0},{5,1},{6,2},{7,3},{8,12},{9,13},{10,... | collective-permute-start | bytes 135176 | tf_op jit(solution)/shard_map/ppermute | solution.py:304
  41.9 10.9 %collective-permute-start.7 = (bf16[144,2048]{1,0:T(8,128)(2,1)S(1)}, bf16[144,2048]{1,0:T(8,128)(2,1)S(1)}, u32[]{:S(2)}, u32[]{:S(2)}) collective-permute-start(bf16[144,2048]{1,0:T(8,128)(2,1)S(1)} %get-tuple-element.107), channel_id=1, source_target_pairs={{0,1},{1,0},{2,3},{3,2},{4,5},{5,4},{6,7},{7,6},{8,9},{9,8},{10,11... | collective-permute-start | bytes 1769480 | tf_op jit(solution)/shard_map/ppermute | solution.py:304
  47.9 4.1 %collective-permute-start.4 = (bf16[176,128]{1,0:T(8,128)(2,1)S(1)}, bf16[176,128]{1,0:T(8,128)(2,1)S(1)}, u32[]{:S(2)}, u32[]{:S(2)}) collective-permute-start(bf16[176,128]{1,0:T(8,128)(2,1)S(1)} %get-tuple-element.97.cur_ref), channel_id=1, source_target_pairs={{0,8},{1,9},{2,10},{3,11},{4,12},{5,13},{6,14},{7,15},{8,0},{9,1},... | collective-permute-start | bytes 135176 | tf_op jit(solution)/shard_map/ppermute | solution.py:304
  48.0 14.1 %collective-permute-start.9 = (bf16[144,2048]{1,0:T(8,128)(2,1)S(1)}, bf16[144,2048]{1,0:T(8,128)(2,1)S(1)}, u32[]{:S(2)}, u32[]{:S(2)}) collective-permute-start(bf16[144,2048]{1,0:T(8,128)(2,1)S(1)} %get-tuple-element.114), channel_id=1, source_target_pairs={{0,1},{1,0},{2,3},{3,2},{4,5},{5,4},{6,7},{7,6},{8,9},{9,8},{10,11... | collective-permute-start | bytes 1769480 | tf_op jit(solution)/shard_map/ppermute | solution.py:304
  52.6 16.7 %collective-permute-start.11 = (bf16[144,2048]{1,0:T(8,128)(2,1)S(1)}, bf16[144,2048]{1,0:T(8,128)(2,1)S(1)}, u32[]{:S(2)}, u32[]{:S(2)}) collective-permute-start(bf16[144,2048]{1,0:T(8,128)(2,1)S(1)} %get-tuple-element.121), channel_id=1, source_target_pairs={{0,1},{1,0},{2,3},{3,2},{4,5},{5,4},{6,7},{7,6},{8,9},{9,8},{10,11... | collective-permute-start | bytes 1769480 | tf_op jit(solution)/shard_map/ppermute | solution.py:304
  52.6 5.6 %collective-permute-start.6 = (bf16[176,128]{1,0:T(8,128)(2,1)S(1)}, bf16[176,128]{1,0:T(8,128)(2,1)S(1)}, u32[]{:S(2)}, u32[]{:S(2)}) collective-permute-start(bf16[176,128]{1,0:T(8,128)(2,1)S(1)} %get-tuple-element.106.cur_ref), channel_id=1, source_target_pairs={{0,16},{1,17},{2,18},{3,19},{4,20},{5,21},{6,22},{7,23},{8,24},{9,... | collective-permute-start | bytes 135176 | tf_op jit(solution)/shard_map/ppermute | solution.py:304
  58.7 9.9 %collective-permute-start.8 = (bf16[176,128]{1,0:T(8,128)(2,1)S(1)}, bf16[176,128]{1,0:T(8,128)(2,1)S(1)}, u32[]{:S(2)}, u32[]{:S(2)}) collective-permute-start(bf16[176,128]{1,0:T(8,128)(2,1)S(1)} %get-tuple-element.113.cur_ref), channel_id=1, source_target_pairs={{0,32},{1,33},{2,34},{3,35},{4,36},{5,37},{6,38},{7,39},{8,40},{9,... | collective-permute-start | bytes 135176 | tf_op jit(solution)/shard_map/ppermute | solution.py:304
  69.2 4.1 %collective-permute-start.10 = (bf16[176,128]{1,0:T(8,128)(2,1)S(1)}, bf16[176,128]{1,0:T(8,128)(2,1)S(1)}, u32[]{:S(2)}, u32[]{:S(2)}) collective-permute-start(bf16[176,128]{1,0:T(8,128)(2,1)S(1)} %get-tuple-element.120.cur_ref), channel_id=1, source_target_pairs={{0,64},{1,65},{2,66},{3,67},{4,68},{5,69},{6,70},{7,71},{8,72},{9,... | collective-permute-start | bytes 135176 | tf_op jit(solution)/shard_map/ppermute | solution.py:304
  73.9 5.6 %collective-permute-start.12 = (bf16[176,128]{1,0:T(8,128)(2,1)S(1)}, bf16[176,128]{1,0:T(8,128)(2,1)S(1)}, u32[]{:S(2)}, u32[]{:S(2)}) collective-permute-start(bf16[176,128]{1,0:T(8,128)(2,1)S(1)} %get-tuple-element.127.cur_ref), channel_id=1, source_target_pairs={{0,128},{1,129},{2,130},{3,131},{4,132},{5,133},{6,134},{7,135},{8... | collective-permute-start | bytes 135176 | tf_op jit(solution)/shard_map/ppermute | solution.py:304
